TPU v7x, 32 devices: a whole 2x2x4 slice. The times are simulated.
32 devices in a mesh: replica: 16 (over z, y, core), fsdp: 2 (over x).
Axes of the slice: x: 2, y: 2, z: 4, core: 2. Of those that a mesh axis runs over, the one named last changes fastest.
Arguments:
- inner_weights: float32 [16, 3, 24, 6144], P('replica', None, None, 'fsdp'), may hold values from -8 to 8
- anchor: float32 [3, 24, 6144], P(None, None, 'fsdp'), may hold values from -4 to 4
- outer_moment: float32 [3, 24, 6144], P(None, None, 'fsdp'), may hold values from -3 to 3
- adam_first: float32 [16, 3, 24, 6144], P('replica', None, None, 'fsdp'), may hold values from -2 to 2
- adam_second: float32 [16, 3, 24, 6144], P('replica', None, None, 'fsdp'), may hold values from 0.1 to 1
- grad_parts: bfloat16 [16, 2, 3, 24, 6144], P('replica', 'fsdp'), may hold values from -2.5 to 2.5
Outputs:
- fresh_weights: bfloat16 [3, 24, 6144], replicated
- anchor_new: float32 [3, 24, 6144], P(None, None, 'fsdp')
- moment_new: float32 [3, 24, 6144], P(None, None, 'fsdp')
- first_new: float32 [16, 3, 24, 6144], P('replica', None, None, 'fsdp')
- second_new: float32 [16, 3, 24, 6144], P('replica', None, None, 'fsdp')
All inputs are finite; a program needn't handle non-finite values.
Results may differ from a plain program's by a relative error of at most 0.0025.
Values may be sent and summed in bfloat16 or wider, within the bound.
A program may use at most 64 MiB of HBM per device.

v0:
```python
import jax
import jax.numpy as jnp
from jax import lax
from jax.sharding import PartitionSpec as P

beta_one = 0.9
beta_two = 0.95
correct_one = 0.99997343860111
correct_two = 0.994079470779666
adam_eps = 1e-08
inner_rate = 0.1
decay_rate = 0.1
outer_rate = 0.7
outer_mu = 0.9


def inner_update(weights, anchor_now, first_now, second_now, gradient):
    first_new = beta_one * first_now + (1.0 - beta_one) * gradient
    second_new = beta_two * second_now + (1.0 - beta_two) * gradient * gradient
    update = first_new / correct_one / (jnp.sqrt(second_new / correct_two) + adam_eps)
    stepped = weights - inner_rate * (update + decay_rate * weights)
    return (first_new, second_new, anchor_now - stepped)


def outer_update(mean_delta, moment_now, anchor_now):
    moment_new = outer_mu * moment_now + mean_delta
    anchor_new = anchor_now - outer_rate * (mean_delta + outer_mu * moment_new)
    return (moment_new, anchor_new)


def per_device(inner_weights, anchor, outer_moment, adam_first, adam_second, grad_parts):
    received = lax.all_to_all(grad_parts, "fsdp", split_axis=4, concat_axis=1, tiled=True)
    gradient = jnp.sum(received.astype(jnp.float32), axis=1)
    first_new, second_new, pseudo = inner_update(
        inner_weights, anchor[None], adam_first, adam_second, gradient
    )
    pseudo = pseudo[0]
    workers = lax.axis_size("replica")
    summed = lax.psum(pseudo, "replica")
    moment_new, anchor_new = outer_update(summed / workers, outer_moment, anchor)
    fresh_weights = lax.all_gather(anchor_new.astype(jnp.bfloat16), "fsdp", axis=2, tiled=True)
    return (fresh_weights, anchor_new, moment_new, first_new, second_new)


def solution(mesh):
    in_specs = (
        P("replica", None, None, "fsdp"),
        P(None, None, "fsdp"),
        P(None, None, "fsdp"),
        P("replica", None, None, "fsdp"),
        P("replica", None, None, "fsdp"),
        P("replica", "fsdp", None, None, None),
    )
    out_specs = (
        P(),
        P(None, None, "fsdp"),
        P(None, None, "fsdp"),
        P("replica", None, None, "fsdp"),
        P("replica", None, None, "fsdp"),
    )
    return jax.shard_map(
        per_device, mesh=mesh, in_specs=in_specs, out_specs=out_specs, check_vma=False
    )
```

profile of v0, /device:TPU:0, one launch (start us, length us, event | category | flops | bytes accessed | tf_op | source)
XLA Modules:
  0.0 183.9 jit_solution(3862538814976636377)
XLA Ops:
  7.2 0.0 all-reduce.2.cloned.1.call-start
  7.2 8.0 %copy.50 = bf16[1,1,3,24,6144]{3,2,1,0,4:T(4,128)(2,1)} copy(bf16[1,1,3,24,6144]{4,3,2,1,0:T(8,128)(2,1)} %param.11) | data formatting | bytes 1769472 | tf_op args[5]
  15.3 8.1 %reshape.49 = bf16[2,2,110592]{2,1,0:T(2,128)(2,1)S(1)} reshape(bf16[6144,1,1,3,24]{4,3,2,1,0:T(4,128)(2,1)} %bitcast.18) | data formatting | bytes 1769472
  23.4 15.9 %all_to_all.4 = bf16[2,2,110592]{2,1,0:T(2,128)(2,1)S(1)} all-to-all(bf16[2,2,110592]{2,1,0:T(2,128)(2,1)S(1)} %reshape.49), channel_id=1, replica_groups=mesh['replica'=16,'fsdp'=2] {'fsdp'}, dimensions={0} | all-to-all | bytes 1769472 | tf_op jit(solution)/shard_map/all_to_all | solution.py:32
  39.3 8.9 %reshape.50 = bf16[6144,1,1,3,24]{4,3,2,1,0:T(4,128)(2,1)} reshape(bf16[2,2,110592]{2,1,0:T(2,128)(2,1)S(1)} %all_to_all.4) | data formatting | bytes 1769472
  48.1 11.1 %convert_reduce_fusion = f32[3,24,3072]{1,0,2:T(4,128)} fusion(bf16[3,24,2,3072]{1,0,3,2:T(4,128)(2,1)} %bitcast.17), kind=kLoop, calls=%fused_computation | loop fusion | flops 663552 | bytes 1769472 | tf_op jit(solution)/shard_map/reduce_sum | solution.py:33
  59.2 0.0 copy-start
  59.2 0.0 copy-start.1
  59.2 0.0 copy-start.2
  59.2 5.1 %copy.51 = f32[3,24,3072]{2,1,0:T(8,128)S(1)} copy(f32[3,24,3072]{1,0,2:T(4,128)} %convert_reduce_fusion) | data formatting | bytes 1769472 | tf_op jit(solution)/shard_map/reduce_sum | solution.py:33
  64.3 0.0 copy-done
  64.3 0.0 copy-done.1
  64.4 0.0 copy-done.2
  64.4 3.1 %fusion.2 = (f32[3,24,3072]{2,1,0:T(8,128)}, f32[1,3,24,3072]{3,2,1,0:T(8,128)}, f32[1,3,24,3072]{3,2,1,0:T(8,128)}) fusion(f32[3,24,3072]{2,1,0:T(8,128)S(1)} %copy-done, f32[1,3,24,3072]{3,2,1,0:T(8,128)S(1)} %copy-done.1, f32[3,24,3072]{2,1,0:T(8,128)S(1)} %copy.51, f32[1,3,24,3072]{3,2,1,0:T(8,128)S(1)} %copy-done.2, f32[1,3,24,3072]{3,2,1,0:T(8,128)} %param.10), kind=kLoop, calls=%fused_computation.6 | loop fusion | flops 3538944 | bytes 7077888 | tf_op jit(solution)/shard_map/squeeze | solution.py:37
  67.5 0.0 all-reduce.2.cloned.1.call-update
  67.5 94.0 %all-reduce.2.cloned.1.call-done = f32[3,24,3072]{2,1,0:T(8,128)} async-done(((f32[3,24,3072]{2,1,0:T(8,128)}), f32[3,24,3072]{2,1,0:T(8,128)}) %all-reduce.2.cloned.1.call-update) | async-done | bytes 884752 | tf_op jit(solution)/shard_map/psum | solution.py:39
  161.5 2.9 %fusion.3 = (bf16[3,24,3072]{2,1,0:T(8,128)(2,1)S(1)}, f32[3,24,3072]{2,1,0:T(8,128)}, f32[3,24,3072]{2,1,0:T(8,128)}) fusion(f32[3,24,3072]{2,1,0:T(8,128)S(1)} %copy-done, f32[3,24,3072]{2,1,0:T(8,128)} %all-reduce.2.cloned.1.call-done, f32[3,24,3072]{2,1,0:T(8,128)} %param.8), kind=kLoop, calls=%fused_computation.9 | loop fusion | flops 1769472 | bytes 4866048 | tf_op jit(solution)/shard_map/convert_element_type | solution.py:41
  164.4 11.7 %all_gather.3 = bf16[3,24,6144]{2,1,0:T(8,128)(2,1)S(1)} all-gather(bf16[3,24,3072]{2,1,0:T(8,128)(2,1)S(1)} %get-tuple-element.15), channel_id=1, replica_groups=mesh['replica'=16,'fsdp'=2] {'fsdp'}, dimensions={2}, use_global_device_ids=true | all-gather | bytes 1327104 | tf_op jit(solution)/shard_map/all_gather | solution.py:41
  176.1 0.9 copy.54
Async XLA Ops:
  7.2 154.3 %all-reduce.2.cloned.1.call-start = ((), (), s32[]{:S(2)}) async-start(), calls=%async_computation.1 | async-start | bytes 1769472 | tf_op jit(solution)/shard_map/psum | solution.py:39
  59.2 5.1 %copy-start = (f32[3,24,3072]{2,1,0:T(8,128)S(1)}, f32[3,24,3072]{2,1,0:T(8,128)}, u32[]{:S(2)}) copy-start(f32[3,24,3072]{2,1,0:T(8,128)} %param.7) | copy-start | bytes 2654212
  59.2 5.1 %copy-start.1 = (f32[1,3,24,3072]{3,2,1,0:T(8,128)S(1)}, f32[1,3,24,3072]{3,2,1,0:T(8,128)}, u32[]{:S(2)}) copy-start(f32[1,3,24,3072]{3,2,1,0:T(8,128)} %param.6) | copy-start | bytes 2654212
  59.2 5.1 %copy-start.2 = (f32[1,3,24,3072]{3,2,1,0:T(8,128)S(1)}, f32[1,3,24,3072]{3,2,1,0:T(8,128)}, u32[]{:S(2)}) copy-start(f32[1,3,24,3072]{3,2,1,0:T(8,128)} %param.9) | copy-start | bytes 2654212
Sparse Core Ops, SparseCore 0:
  67.6 93.8 all-reduce.1
where the time goes:
time: 185 us; the launch traced here: 184 us
  waiting for transfers between devices  94 us (51%)
  local copies, waits for them, and re-layouts  31.1 us (17%)
  blocking collectives  27.6 us (15%)
  other arithmetic  17.1 us (9%)
  between operations  14.1 us (8%)
    psum x1, waiting for transfers between devices, per_device(): summed = lax.psum(pseudo, 'replica')  94 us
    unnamed x10, local copies, waits for them, and re-layouts  26 us
    all_to_all x1, blocking collectives, per_device(): lax.all_to_all(grad_parts, 'fsdp', split_axis=4, concat_axis=1, tiled=True)  15.9 us
    all_gather x1, blocking collectives, per_device(): lax.all_gather(anchor_new.astype(jnp.bfloat16), 'fsdp', axis=2, tiled=True)  11.7 us
    reduce_sum x1, other arithmetic, per_device(): gradient = jnp.sum(received.astype(jnp.float32), axis=1)  11.1 us
    reduce_sum x1, local copies, waits for them, and re-layouts, per_device(): gradient = jnp.sum(received.astype(jnp.float32), axis=1)  5.09 us
  transfers between devices with their start and end apart: 1, of which 1 were waited for; matrix products, arithmetic and copies ran while one was open for 0% of the time, Pallas kernels for 0%

commit v1 on v0

--- a/solution.py
+++ b/solution.py
@@ -36,7 +36,7 @@
     )
     pseudo = pseudo[0]
     workers = lax.axis_size("replica")
-    summed = lax.psum(pseudo, "replica")
+    summed = jnp.sum(lax.all_gather(pseudo, "replica"), axis=0)
     moment_new, anchor_new = outer_update(summed / workers, outer_moment, anchor)
     fresh_weights = lax.all_gather(anchor_new.astype(jnp.bfloat16), "fsdp", axis=2, tiled=True)
     return (fresh_weights, anchor_new, moment_new, first_new, second_new)

time: 185 us -> 207 us (1.12)
  waiting for transfers between devices: 94 us -> 111 us
  other arithmetic: 17.1 us -> 21.7 us
    all_gather x0 -> x1, waiting for transfers between devices: none -> 111 us  [per_device(): summed = jnp.sum(lax.all_gather(pseudo, 'replica'), axis=0)]
    psum x1 -> x0, waiting for transfers between devices: 94 us -> none  [per_device(): summed = lax.psum(pseudo, 'replica')]
    reduce_sum x0 -> x1, other arithmetic: none -> 6.05 us  [per_device(): summed = jnp.sum(lax.all_gather(pseudo, 'replica'), axis=0)]
    squeeze x1 -> x0, other arithmetic: 3.11 us -> none  [per_device(): pseudo = pseudo[0]]
    sub x0 -> x1, other arithmetic: none -> 3.11 us  [inner_update(): return (first_new, second_new, anchor_now - stepped)]
    unnamed x10 -> x12, local copies, waits for them, and re-layouts: 26 us -> 26 us
where the time goes in v1:
time: 207 us; the launch traced here: 206 us
  waiting for transfers between devices  111 us (54%)
  local copies, waits for them, and re-layouts  31.1 us (15%)
  blocking collectives  28.9 us (14%)
  other arithmetic  21.7 us (10%)
  between operations  14.1 us (7%)
    all_gather x1, waiting for transfers between devices, per_device(): summed = jnp.sum(lax.all_gather(pseudo, 'replica'), axis=0)  111 us
    unnamed x12, local copies, waits for them, and re-layouts  26 us
    all_to_all x1, blocking collectives, per_device(): lax.all_to_all(grad_parts, 'fsdp', split_axis=4, concat_axis=1, tiled=True)  16 us
    all_gather x1, blocking collectives, per_device(): lax.all_gather(anchor_new.astype(jnp.bfloat16), 'fsdp', axis=2, tiled=True)  13 us
    reduce_sum x1, other arithmetic, per_device(): gradient = jnp.sum(received.astype(jnp.float32), axis=1)  11.1 us
    reduce_sum x1, other arithmetic, per_device(): summed = jnp.sum(lax.all_gather(pseudo, 'replica'), axis=0)  6.05 us
    reduce_sum x1, local copies, waits for them, and re-layouts, per_device(): gradient = jnp.sum(received.astype(jnp.float32), axis=1)  5.09 us
  transfers between devices with their start and end apart: 1, of which 1 were waited for; matrix products, arithmetic and copies ran while one was open for 0% of the time, Pallas kernels for 0%

profile of v1, /device:TPU:0, one launch (start us, length us, event | category | flops | bytes accessed | tf_op | source)
XLA Modules:
  0.0 206.5 jit_solution(5544960593438542141)
XLA Ops:
  7.2 0.0 all-gather.2.cloned.1.call-start
  7.2 8.1 %copy.26 = bf16[1,1,3,24,6144]{3,2,1,0,4:T(4,128)(2,1)} copy(bf16[1,1,3,24,6144]{4,3,2,1,0:T(8,128)(2,1)} %param.11) | data formatting | bytes 1769472 | tf_op args[5]
  15.3 8.1 %reshape.49 = bf16[2,2,110592]{2,1,0:T(2,128)(2,1)S(1)} reshape(bf16[6144,1,1,3,24]{4,3,2,1,0:T(4,128)(2,1)} %bitcast.14) | data formatting | bytes 1769472
  23.4 16.0 %all_to_all.4 = bf16[2,2,110592]{2,1,0:T(2,128)(2,1)S(1)} all-to-all(bf16[2,2,110592]{2,1,0:T(2,128)(2,1)S(1)} %reshape.49), channel_id=1, replica_groups=mesh['replica'=16,'fsdp'=2] {'fsdp'}, dimensions={0} | all-to-all | bytes 1769472 | tf_op jit(solution)/shard_map/all_to_all | solution.py:32
  39.4 8.8 %reshape.50 = bf16[6144,1,1,3,24]{4,3,2,1,0:T(4,128)(2,1)} reshape(bf16[2,2,110592]{2,1,0:T(2,128)(2,1)S(1)} %all_to_all.4) | data formatting | bytes 1769472
  48.2 11.1 %convert_reduce_fusion = f32[3,24,3072]{1,0,2:T(4,128)} fusion(bf16[3,24,2,3072]{1,0,3,2:T(4,128)(2,1)} %bitcast.13), kind=kLoop, calls=%fused_computation | loop fusion | flops 663552 | bytes 1769472 | tf_op jit(solution)/shard_map/reduce_sum | solution.py:33
  59.3 0.0 copy-start
  59.3 0.0 copy-start.1
  59.3 0.0 copy-start.2
  59.3 5.1 %copy.27 = f32[3,24,3072]{2,1,0:T(8,128)S(1)} copy(f32[3,24,3072]{1,0,2:T(4,128)} %convert_reduce_fusion) | data formatting | bytes 1769472 | tf_op jit(solution)/shard_map/reduce_sum | solution.py:33
  64.4 0.0 copy-done
  64.4 0.0 copy-done.1
  64.4 0.0 copy-done.2
  64.4 3.1 %bitcast_subtract_fusion = (f32[1,3,24,3072]{3,2,1,0:T(8,128)}, f32[1,3,24,3072]{3,2,1,0:T(8,128)}, f32[1,3,24,3072]{3,2,1,0:T(8,128)}) fusion(f32[3,24,3072]{2,1,0:T(8,128)S(1)} %copy-done, f32[1,3,24,3072]{3,2,1,0:T(8,128)S(1)} %copy-done.1, f32[3,24,3072]{2,1,0:T(8,128)S(1)} %copy.27, f32[1,3,24,3072]{3,2,1,0:T(8,128)S(1)} %copy-done.2, ...), kind=kLoop, calls=%fused_computation.5 | loop fusion | flops 3538944 | bytes 7077888 | tf_op jit(solution)/shard_map/sub | solution.py:22
  67.5 0.0 all-gather.2.cloned.1.call-update
  67.6 0.0 copy-start.3
  67.6 110.6 %all-gather.2.cloned.1.call-done = f32[16,3,24,3072]{3,2,1,0:T(8,128)} async-done(((f32[1,3,24,3072]{3,2,1,0:T(8,128)}), f32[16,3,24,3072]{3,2,1,0:T(8,128)}) %all-gather.2.cloned.1.call-update) | async-done | bytes 14155792 | tf_op jit(solution)/shard_map/all_gather | solution.py:39
  178.2 6.0 %reduce_sum.22 = f32[3,24,3072]{2,1,0:T(8,128)S(1)} reduce(f32[16,3,24,3072]{3,2,1,0:T(8,128)} %all-gather.2.cloned.1.call-done, f32[]{:T(128)} %constant.3.clone.1), dimensions={0}, to_apply=%region_1.0 | reduce | flops 3317760 | bytes 15040516 | tf_op jit(solution)/shard_map/reduce_sum | solution.py:39
  184.3 0.0 copy-done.3
  184.3 1.5 fusion.2
  185.7 13.0 %all_gather.7 = bf16[3,24,6144]{2,1,0:T(8,128)(2,1)S(1)} all-gather(bf16[3,24,3072]{2,1,0:T(8,128)(2,1)S(1)} %get-tuple-element.10), channel_id=1, replica_groups=mesh['replica'=16,'fsdp'=2] {'fsdp'}, dimensions={2}, use_global_device_ids=true | all-gather | bytes 1327104 | tf_op jit(solution)/shard_map/all_gather | solution.py:41
  198.7 0.9 copy.29
Async XLA Ops:
  7.2 171.1 %all-gather.2.cloned.1.call-start = ((), (), s32[]{:S(2)}) async-start(), calls=%async_computation.1 | async-start | bytes 15040512 | tf_op jit(solution)/shard_map/all_gather | solution.py:39
  59.3 5.1 %copy-start = (f32[3,24,3072]{2,1,0:T(8,128)S(1)}, f32[3,24,3072]{2,1,0:T(8,128)}, u32[]{:S(2)}) copy-start(f32[3,24,3072]{2,1,0:T(8,128)} %param.7) | copy-start | bytes 2654212
  59.3 5.1 %copy-start.1 = (f32[1,3,24,3072]{3,2,1,0:T(8,128)S(1)}, f32[1,3,24,3072]{3,2,1,0:T(8,128)}, u32[]{:S(2)}) copy-start(f32[1,3,24,3072]{3,2,1,0:T(8,128)} %param.6) | copy-start | bytes 2654212
  59.3 5.1 %copy-start.2 = (f32[1,3,24,3072]{3,2,1,0:T(8,128)S(1)}, f32[1,3,24,3072]{3,2,1,0:T(8,128)}, u32[]{:S(2)}) copy-start(f32[1,3,24,3072]{3,2,1,0:T(8,128)} %param.9) | copy-start | bytes 2654212
  67.6 116.7 %copy-start.3 = (f32[3,24,3072]{2,1,0:T(8,128)S(1)}, f32[3,24,3072]{2,1,0:T(8,128)}, u32[]{:S(2)}) copy-start(f32[3,24,3072]{2,1,0:T(8,128)} %param.8) | copy-start | bytes 2654212
Sparse Core Ops, SparseCore 0:
  67.7 110.4 all-gather.1
